TPU v7x, 32 devices: a whole 2x2x4 slice. The times are simulated.
32 devices in a mesh: rows: 4 (over z), cent: 8 (over y, x, core).
Axes of the slice: x: 2, y: 2, z: 4, core: 2. Of those that a mesh axis runs over, the one named last changes fastest.
Arguments:
- train_rows: float32 [16384, 64], P('rows'), may hold values from -6 to 6
- centre_index: int32 [16384], P('cent'), may hold values from 0 to 16383
- precond: bfloat16 [16384, 16384], P('cent', 'rows'), as said below
- coefficients: float32 [16384, 128], P(('rows', 'cent')), may hold values from -6 to 6
- residual: float32 [16384, 128], P(('rows', 'cent')), may hold values from -6 to 6
- direction: float32 [16384, 128], P(('rows', 'cent')), may hold values from -6 to 6
Outputs:
- coef_next: float32 [16384, 128], P(('rows', 'cent'))
- residual_next: float32 [16384, 128], P(('rows', 'cent'))
- direction_next: float32 [16384, 128], P(('rows', 'cent'))
Inputs may be any that keep to these rules, and one draw needn't show every extreme that they name: precond is zero below its diagonal.
All inputs are finite; a program needn't handle non-finite values.
Results may differ from a plain program's by a relative error of at most 0.0047.
Values may be sent and summed in bfloat16 or wider, within the bound.
A program may use at most 128 MiB of HBM per device.

v0:
```python
import math
import jax
import jax.numpy as jnp
from jax import lax
from jax.sharding import PartitionSpec as P

FEAT = 64
OUTS = 128
ridge_weight = 0.1


def kernel_tile(block_rows, centres):
    row_sq = jnp.sum(block_rows * block_rows, axis=1)
    cen_sq = jnp.sum(centres * centres, axis=1)
    cross = jnp.dot(
        block_rows, centres.T, precision=lax.Precision.HIGHEST, preferred_element_type=jnp.float32
    )
    distance = row_sq[:, None] + cen_sq[None, :] - 2.0 * cross
    return jnp.exp(-(2.0 / FEAT) * distance).astype(jnp.bfloat16)


def kernel_pass(local_rows, centres, coef_field, combine):
    count_rows = local_rows.shape[0]
    block_size = math.gcd(count_rows, 1024)
    block_count = count_rows // block_size
    groups = local_rows.reshape(block_count, block_size, FEAT)
    tiles = lax.map(lambda group_rows: kernel_tile(group_rows, centres), groups)
    fitted_part = jnp.einsum(
        "kbc,cd->kbd", tiles, coef_field, preferred_element_type=jnp.float32
    ).reshape(count_rows, OUTS)
    fitted = combine(fitted_part)
    fitted_groups = fitted.reshape(block_count, block_size, OUTS)
    grad_part = jnp.einsum("kbc,kbd->cd", tiles, fitted_groups, preferred_element_type=jnp.float32)
    return grad_part


def on_device(train_rows, centre_index, precond, coefficients, residual, direction):
    rows_here = train_rows.shape[0]
    start_row = lax.axis_index("rows") * rows_here
    offset = centre_index - start_row
    inside = ((offset >= 0) & (offset < rows_here)).astype(jnp.float32)
    picked = train_rows[jnp.clip(offset, 0, rows_here - 1)] * inside[:, None]
    centres = lax.psum(picked, "rows")
    dir_low = direction.astype(jnp.bfloat16)
    columns = precond
    partial_field = jnp.dot(
        columns,
        lax.all_gather(dir_low, "cent", axis=0, tiled=True),
        preferred_element_type=jnp.float32,
    )
    coef_field = lax.psum(partial_field, "rows").astype(jnp.bfloat16)

    def line_sum(part):
        return lax.psum(part, "cent").astype(jnp.bfloat16)

    grad_part = kernel_pass(train_rows, centres, coef_field, line_sum)
    grad = lax.psum(grad_part, "rows")
    grad_low = (grad * float(rows_here * lax.axis_size("rows")) ** (-0.5)).astype(jnp.bfloat16)
    columns = precond
    image = lax.psum_scatter(
        lax.dot_general(
            columns, grad_low, (((0,), (0,)), ((), ())), preferred_element_type=jnp.float32
        ),
        "cent",
        scatter_dimension=0,
        tiled=True,
    )
    image = image + ridge_weight * direction
    norm_old, curvature = lax.psum(
        (jnp.sum(residual * residual), jnp.sum(direction * image)), ("rows", "cent")
    )
    step_size = norm_old / curvature
    coef_next = coefficients + step_size * direction
    residual_next = residual - step_size * image
    norm_new = lax.psum(jnp.sum(residual_next * residual_next), ("rows", "cent"))
    direction_next = residual_next + norm_new / norm_old * direction
    return (coef_next, residual_next, direction_next)


def solution(mesh):
    placed = (
        P("rows", None),
        P("cent"),
        P("cent", "rows"),
        P(("rows", "cent"), None),
        P(("rows", "cent"), None),
        P(("rows", "cent"), None),
    )
    return jax.shard_map(
        on_device,
        mesh=mesh,
        in_specs=placed,
        out_specs=(P(("rows", "cent"), None), P(("rows", "cent"), None), P(("rows", "cent"), None)),
        check_vma=False,
    )
```

profile of v0, /device:TPU:0, one launch (start us, length us, event | category | flops | bytes accessed | tf_op | source)
XLA Modules:
  0.0 441.2 jit_solution(3471181950002680406)
XLA Ops:
  9.5 1.8 copy.9
  11.3 5.5 %gather_fusion = f32[2048,64]{1,0:T(8,128)S(1)} fusion(f32[4096,64]{1,0:T(8,128)S(1)} %copy.9, s32[2048]{0:T(1024)S(1)} %fusion.8), kind=kCustom, calls=%fused_computation | custom fusion | bytes 1056768 | tf_op jit(solution)/shard_map/gather | solution.py:42
  16.8 1.3 broadcast_multiply_fusion
  18.2 1.6 convert_element_type.21
  19.9 53.0 %all-reduce.6.cloned.1.call-done = f32[2048,64]{1,0:T(8,128)} async-done(((f32[2048,64]{1,0:T(8,128)}), f32[2048,64]{1,0:T(8,128)}) %all-reduce.6.cloned.1.call-update) | async-done | bytes 524304 | tf_op jit(solution)/shard_map/psum | solution.py:43
  72.9 1.6 multiply_reduce_fusion
  74.5 45.0 %while.12 = (s32[]{:T(128)}, bf16[4,1024,2048]{2,1,0:T(8,128)(2,1)}, f32[4,1024,64]{2,1,0:T(8,128)S(1)}, f32[2048]{0:T(1024)S(1)}, f32[2048,64]{1,0:T(8,128)}, /*index=5*/s32[]{:T(128)}) while((s32[]{:T(128)}, bf16[4,1024,2048]{2,1,0:T(8,128)(2,1)}, f32[4,1024,64]{2,1,0:T(8,128)S(1)}, f32[2048]{0:T(1024)S(1)}, f32[2048,64]{1,0:T(8,128)}, ...), condition=%wide.region_6.7_spmd, body=%wide.region_4.0_spmd.sunk | while | flops 1621228544 | bytes 6046793 | solution.py:27
  74.7 11.0 %bitcast_dynamic-update-slice_fusion.2 = bf16[4,1024,2048]{2,1,0:T(8,128)(2,1)} fusion(bf16[4,1024,2048]{2,1,0:T(8,128)(2,1)} %get-tuple-element.116, s32[]{:T(128)} %get-tuple-element.115, f32[2048,64]{1,0:T(8,128)} %get-tuple-element.125, f32[2048]{0:T(1024)S(1)} %get-tuple-element.124, f32[1024]{0:T(1024)S(1)} %fusion.23, ...), kind=kOutput, calls=%fused_computation.2.clone.1 | convolution fusion | flops 1621098496 | bytes 5780480 | tf_op jit(solution)/shard_map/while/body/eval_jaxpr/dot_general | solution.py:15
  85.9 11.1 %bitcast_dynamic-update-slice_fusion.2 = bf16[4,1024,2048]{2,1,0:T(8,128)(2,1)} fusion(bf16[4,1024,2048]{2,1,0:T(8,128)(2,1)} %get-tuple-element.116, s32[]{:T(128)} %get-tuple-element.115, f32[2048,64]{1,0:T(8,128)} %get-tuple-element.125, f32[2048]{0:T(1024)S(1)} %get-tuple-element.124, f32[1024]{0:T(1024)S(1)} %fusion.23, ...), kind=kOutput, calls=%fused_computation.2.clone.1 | convolution fusion | flops 1621098496 | bytes 5780480 | tf_op jit(solution)/shard_map/while/body/eval_jaxpr/dot_general | solution.py:15
  97.2 11.0 %bitcast_dynamic-update-slice_fusion.2 = bf16[4,1024,2048]{2,1,0:T(8,128)(2,1)} fusion(bf16[4,1024,2048]{2,1,0:T(8,128)(2,1)} %get-tuple-element.116, s32[]{:T(128)} %get-tuple-element.115, f32[2048,64]{1,0:T(8,128)} %get-tuple-element.125, f32[2048]{0:T(1024)S(1)} %get-tuple-element.124, f32[1024]{0:T(1024)S(1)} %fusion.23, ...), kind=kOutput, calls=%fused_computation.2.clone.1 | convolution fusion | flops 1621098496 | bytes 5780480 | tf_op jit(solution)/shard_map/while/body/eval_jaxpr/dot_general | solution.py:15
  108.4 11.1 %bitcast_dynamic-update-slice_fusion.2 = bf16[4,1024,2048]{2,1,0:T(8,128)(2,1)} fusion(bf16[4,1024,2048]{2,1,0:T(8,128)(2,1)} %get-tuple-element.116, s32[]{:T(128)} %get-tuple-element.115, f32[2048,64]{1,0:T(8,128)} %get-tuple-element.125, f32[2048]{0:T(1024)S(1)} %get-tuple-element.124, f32[1024]{0:T(1024)S(1)} %fusion.23, ...), kind=kOutput, calls=%fused_computation.2.clone.1 | convolution fusion | flops 1621098496 | bytes 5780480 | tf_op jit(solution)/shard_map/while/body/eval_jaxpr/dot_general | solution.py:15
  119.5 8.4 %fusion.10 = f32[2048,128]{1,0:T(8,128)S(1)} fusion(bf16[2048,4096]{1,0:T(8,128)(2,1)} %param.10, bf16[4096,128]{1,0:T(8,128)(2,1)} %all-gather.2.cloned.1.call-done), kind=kOutput, calls=%fused_computation.28 | convolution fusion | flops 2147483648 | bytes 18874368 | tf_op jit(solution)/shard_map/dot_general | solution.py:46
  127.9 41.5 %all-reduce.9 = bf16[2048,128]{1,0:T(8,128)(2,1)S(1)} all-reduce(f32[2048,128]{1,0:T(8,128)S(1)} %fusion.10), channel_id=1, replica_groups=mesh['rows'=4,'cent'=8] {'rows'}, use_global_device_ids=true, to_apply=%region_7.8 | all-reduce | flops 262144 | bytes 1572864 | tf_op jit(solution)/shard_map/psum | solution.py:51
  169.5 8.2 %fusion.4 = f32[4,1024,128]{2,1,0:T(8,128)S(1)} fusion(bf16[4,1024,2048]{2,1,0:T(8,128)(2,1)} %get-tuple-element.58, bf16[2048,128]{1,0:T(8,128)(2,1)S(1)} %all-reduce.9), kind=kOutput, calls=%fused_computation.12 | convolution fusion | flops 2147483648 | bytes 19398656 | tf_op jit(solution)/shard_map/kbc,cd->kbd/dot_general | solution.py:28
  177.6 56.6 %all-reduce.10 = bf16[4096,128]{1,0:T(8,128)(2,1)S(1)} all-reduce(f32[4096,128]{1,0:T(8,128)S(1)} %bitcast.34), channel_id=1, replica_groups=mesh['rows'=4,'cent'=8] {'cent'}, use_global_device_ids=true, to_apply=%region_8.9 | all-reduce | flops 524288 | bytes 3145728 | tf_op jit(solution)/shard_map/psum | solution.py:54
  234.2 9.2 %convolution_bitcast_fusion.1 = f32[2048,128]{1,0:T(8,128)} fusion(bf16[4,1024,2048]{2,1,0:T(8,128)(2,1)} %get-tuple-element.58, bf16[4,1024,128]{2,1,0:T(8,128)(2,1)S(1)} %bitcast.35), kind=kOutput, calls=%fused_computation.9 | convolution fusion | flops 2147483648 | bytes 18874368 | tf_op jit(solution)/shard_map/kbc,kbd->cd/dot_general | solution.py:33
  243.5 50.6 %all-reduce.8.cloned.1.call-done = f32[2048,128]{1,0:T(8,128)} async-done(((f32[2048,128]{1,0:T(8,128)}), f32[2048,128]{1,0:T(8,128)}) %all-reduce.8.cloned.1.call-update) | async-done | bytes 1048592 | tf_op jit(solution)/shard_map/psum | solution.py:57
  294.0 9.8 %convolution_bitcast_fusion = f32[4096,128]{0,1:T(8,128)} fusion(bf16[2048,4096]{1,0:T(8,128)(2,1)} %param.10, f32[2048,128]{1,0:T(8,128)} %all-reduce.8.cloned.1.call-done), kind=kOutput, calls=%fused_computation.8 | convolution fusion | flops 2148007936 | bytes 19922944 | tf_op jit(solution)/shard_map/dot_general | solution.py:61
  304.8 39.4 %reduce-scatter.2.cloned.1.call-done = f32[512,128]{0,1:T(8,128)} async-done(((f32[4096,128]{0,1:T(8,128)}), f32[512,128]{0,1:T(8,128)}) %reduce-scatter.2.cloned.1.call-update) | async-done | bytes 262160 | tf_op jit(solution)/shard_map/reduce_scatter | solution.py:60
  344.2 1.6 multiply_reduce_fusion.2
  346.0 39.6 %all-reduce = (f32[]{:T(128)}, f32[]{:T(128)}) all-reduce(f32[]{:T(128)} %multiply_reduce_fusion.3, f32[]{:T(128)} %multiply_reduce_fusion.2), channel_id=1, replica_groups=mesh['rows'=4,'cent'=8] {'rows','cent'}, use_global_device_ids=true, to_apply=%region_1.2 | all-reduce | flops 2 | bytes 16 | tf_op jit(solution)/shard_map/psum | solution.py:69
  386.9 1.6 multiply_reduce_fusion.1
  388.6 41.3 %psum.55 = f32[]{:T(128)} all-reduce(f32[]{:T(128)} %get-tuple-element.74), channel_id=1, replica_groups=mesh['rows'=4,'cent'=8] {'rows','cent'}, use_global_device_ids=true, to_apply=%region_14.15 | all-reduce | flops 1 | bytes 8 | tf_op jit(solution)/shard_map/psum | solution.py:75
  432.1 0.8 copy.17
  (29 shorter events, 5.3 us)
Async XLA Ops:
  8.0 64.9 %all-reduce.6.cloned.1.call-start = ((), (), s32[]{:S(2)}) async-start(), calls=%async_computation.1 | async-start | bytes 2097152 | tf_op jit(solution)/shard_map/psum | solution.py:43
  18.1 101.4 %all-gather.2.cloned.1.call-start = ((), (), s32[]{:S(2)}) async-start(), calls=%async_computation.2 | async-start | bytes 1179648 | tf_op jit(solution)/shard_map/all_gather | solution.py:48
  19.8 274.2 %all-reduce.8.cloned.1.call-start = ((), (), s32[]{:S(2)}) async-start(), calls=%async_computation.3 | async-start | bytes 2097152 | tf_op jit(solution)/shard_map/psum | solution.py:57
  243.4 60.5 %copy-start = (f32[512,128]{1,0:T(8,128)S(1)}, f32[512,128]{1,0:T(8,128)}, u32[]{:S(2)}) copy-start(f32[512,128]{1,0:T(8,128)} %param.13) | copy-start | bytes 786436
  243.4 60.7 %copy-start.1 = (f32[512,128]{1,0:T(8,128)S(1)}, f32[512,128]{1,0:T(8,128)}, u32[]{:S(2)}) copy-start(f32[512,128]{1,0:T(8,128)} %param.12) | copy-start | bytes 786436
  243.4 102.5 %copy-start.2 = (f32[512,128]{1,0:T(8,128)S(1)}, f32[512,128]{1,0:T(8,128)}, u32[]{:S(2)}) copy-start(f32[512,128]{1,0:T(8,128)} %param.11) | copy-start | bytes 786436
  243.4 100.8 %reduce-scatter.2.cloned.1.call-start = ((), (), s32[]{:S(2)}) async-start(), calls=%async_computation.4 | async-start | bytes 2359296 | tf_op jit(solution)/shard_map/reduce_scatter | solution.py:60
Sparse Core Ops, SparseCore 0:
  18.2 54.6 all-reduce.5
  243.5 50.4 all-reduce.7
Sparse Core Ops, SparseCore 1:
  21.1 25.9 all-gather.1
  304.0 40.2 reduce-scatter.1
where the time goes:
time: 442 us; the launch traced here: 441 us
  blocking collectives  179 us (40%)
  waiting for transfers between devices  143 us (32%)
  matrix products  79.7 us (18%)
  between operations  18.3 us (4%)
  other arithmetic  10.7 us (2%)
  local copies, waits for them, and re-layouts  10.2 us (2%)
    psum x1, blocking collectives, line_sum(): return lax.psum(part, 'cent').astype(jnp.bfloat16)  56.6 us
    psum x1, waiting for transfers between devices, on_device(): centres = lax.psum(picked, 'rows')  53 us
    psum x1, waiting for transfers between devices, on_device(): grad = lax.psum(grad_part, 'rows')  50.6 us
    dot_general x4, matrix products, kernel_tile(): jnp.dot(block_rows, centres.T, precision=lax.Precision.HIGHEST, preferred...  44.2 us
    psum x1, blocking collectives, on_device(): coef_field = lax.psum(partial_field, 'rows').astype(jnp.bfloat16)  41.5 us
    psum x1, blocking collectives, on_device(): lax.psum(jnp.sum(residual_next * residual_next), ('rows', 'cent'))  41.3 us
    psum x1, blocking collectives, on_device(): lax.psum((jnp.sum(residual * residual), jnp.sum(direction * image)), ('ro...  39.6 us
    reduce_scatter x1, waiting for transfers between devices, on_device(): lax.psum_scatter(lax.dot_general(columns, grad_low, (((0,), (0,)), ((), (...  39.4 us
  transfers between devices with their start and end apart: 4, of which 3 were waited for; matrix products, arithmetic and copies ran while one was open for 11% of the time, Pallas kernels for 0%

commit v1 on v0

--- a/solution.py
+++ b/solution.py
@@ -67,7 +67,7 @@
     )
     image = image + ridge_weight * direction
     norm_old, curvature = lax.psum(
-        (jnp.sum(residual * residual), jnp.sum(direction * image)), ("rows", "cent")
+        lax.psum((jnp.sum(residual * residual), jnp.sum(direction * image)), "rows"), "cent"
     )
     step_size = norm_old / curvature
     coef_next = coefficients + step_size * direction

time: 442 us -> 424 us (0.959)
  blocking collectives: 179 us -> 160 us
    psum x1 -> x2, blocking collectives: 39.6 us -> 24.8 us  [the longest x1 12.4 us: on_device(): lax.psum(lax.psum((jnp.sum(residual * residual), jnp.sum(direction * imag...]
  transfers between devices with their start and end apart: 4 -> 4, of which waited for: 3 -> 3; matrix products, arithmetic and copies ran while one was open for 11% -> 12% of each run, Pallas kernels for 0% -> 0%
where the time goes in v1:
time: 424 us; the launch traced here: 422 us
  blocking collectives  160 us (38%)
  waiting for transfers between devices  143 us (34%)
  matrix products  79.7 us (19%)
  between operations  18.3 us (4%)
  other arithmetic  10.7 us (3%)
  local copies, waits for them, and re-layouts  10.2 us (2%)
    psum x1, blocking collectives, line_sum(): return lax.psum(part, 'cent').astype(jnp.bfloat16)  56.6 us
    psum x1, waiting for transfers between devices, on_device(): centres = lax.psum(picked, 'rows')  53 us
    psum x1, waiting for transfers between devices, on_device(): grad = lax.psum(grad_part, 'rows')  50.6 us
    dot_general x4, matrix products, kernel_tile(): jnp.dot(block_rows, centres.T, precision=lax.Precision.HIGHEST, preferred...  44.2 us
    psum x1, blocking collectives, on_device(): coef_field = lax.psum(partial_field, 'rows').astype(jnp.bfloat16)  41.5 us
    reduce_scatter x1, waiting for transfers between devices, on_device(): lax.psum_scatter(lax.dot_general(columns, grad_low, (((0,), (0,)), ((), (...  39.4 us
    psum x1, blocking collectives, on_device(): lax.psum(jnp.sum(residual_next * residual_next), ('rows', 'cent'))  37 us
    psum x1, blocking collectives, on_device(): lax.psum(lax.psum((jnp.sum(residual * residual), jnp.sum(direction * imag...  12.4 us
  transfers between devices with their start and end apart: 4, of which 3 were waited for; matrix products, arithmetic and copies ran while one was open for 12% of the time, Pallas kernels for 0%

profile of v1, /device:TPU:0, one launch (start us, length us, event | category | flops | bytes accessed | tf_op | source)
XLA Modules:
  0.0 422.1 jit_solution(12373093432765141799)
XLA Ops:
  9.5 1.8 copy.9
  11.3 5.5 %gather_fusion = f32[2048,64]{1,0:T(8,128)S(1)} fusion(f32[4096,64]{1,0:T(8,128)S(1)} %copy.9, s32[2048]{0:T(1024)S(1)} %fusion.8), kind=kCustom, calls=%fused_computation | custom fusion | bytes 1056768 | tf_op jit(solution)/shard_map/gather | solution.py:42
  16.8 1.3 broadcast_multiply_fusion
  18.2 1.6 convert_element_type.21
  19.9 53.0 %all-reduce.7.cloned.1.call-done = f32[2048,64]{1,0:T(8,128)} async-done(((f32[2048,64]{1,0:T(8,128)}), f32[2048,64]{1,0:T(8,128)}) %all-reduce.7.cloned.1.call-update) | async-done | bytes 524304 | tf_op jit(solution)/shard_map/psum | solution.py:43
  72.9 1.6 multiply_reduce_fusion
  74.5 45.0 %while.12 = (s32[]{:T(128)}, bf16[4,1024,2048]{2,1,0:T(8,128)(2,1)}, f32[4,1024,64]{2,1,0:T(8,128)S(1)}, f32[2048]{0:T(1024)S(1)}, f32[2048,64]{1,0:T(8,128)}, /*index=5*/s32[]{:T(128)}) while((s32[]{:T(128)}, bf16[4,1024,2048]{2,1,0:T(8,128)(2,1)}, f32[4,1024,64]{2,1,0:T(8,128)S(1)}, f32[2048]{0:T(1024)S(1)}, f32[2048,64]{1,0:T(8,128)}, ...), condition=%wide.region_7.8_spmd, body=%wide.region_5.7_spmd.sunk | while | flops 1621228544 | bytes 6046793 | solution.py:27
  74.7 11.0 %bitcast_dynamic-update-slice_fusion.2 = bf16[4,1024,2048]{2,1,0:T(8,128)(2,1)} fusion(bf16[4,1024,2048]{2,1,0:T(8,128)(2,1)} %get-tuple-element.118, s32[]{:T(128)} %get-tuple-element.117, f32[2048,64]{1,0:T(8,128)} %get-tuple-element.127, f32[2048]{0:T(1024)S(1)} %get-tuple-element.126, f32[1024]{0:T(1024)S(1)} %fusion.23, ...), kind=kOutput, calls=%fused_computation.2.clone.1 | convolution fusion | flops 1621098496 | bytes 5780480 | tf_op jit(solution)/shard_map/while/body/eval_jaxpr/dot_general | solution.py:15
  85.9 11.1 %bitcast_dynamic-update-slice_fusion.2 = bf16[4,1024,2048]{2,1,0:T(8,128)(2,1)} fusion(bf16[4,1024,2048]{2,1,0:T(8,128)(2,1)} %get-tuple-element.118, s32[]{:T(128)} %get-tuple-element.117, f32[2048,64]{1,0:T(8,128)} %get-tuple-element.127, f32[2048]{0:T(1024)S(1)} %get-tuple-element.126, f32[1024]{0:T(1024)S(1)} %fusion.23, ...), kind=kOutput, calls=%fused_computation.2.clone.1 | convolution fusion | flops 1621098496 | bytes 5780480 | tf_op jit(solution)/shard_map/while/body/eval_jaxpr/dot_general | solution.py:15
  97.2 11.0 %bitcast_dynamic-update-slice_fusion.2 = bf16[4,1024,2048]{2,1,0:T(8,128)(2,1)} fusion(bf16[4,1024,2048]{2,1,0:T(8,128)(2,1)} %get-tuple-element.118, s32[]{:T(128)} %get-tuple-element.117, f32[2048,64]{1,0:T(8,128)} %get-tuple-element.127, f32[2048]{0:T(1024)S(1)} %get-tuple-element.126, f32[1024]{0:T(1024)S(1)} %fusion.23, ...), kind=kOutput, calls=%fused_computation.2.clone.1 | convolution fusion | flops 1621098496 | bytes 5780480 | tf_op jit(solution)/shard_map/while/body/eval_jaxpr/dot_general | solution.py:15
  108.4 11.1 %bitcast_dynamic-update-slice_fusion.2 = bf16[4,1024,2048]{2,1,0:T(8,128)(2,1)} fusion(bf16[4,1024,2048]{2,1,0:T(8,128)(2,1)} %get-tuple-element.118, s32[]{:T(128)} %get-tuple-element.117, f32[2048,64]{1,0:T(8,128)} %get-tuple-element.127, f32[2048]{0:T(1024)S(1)} %get-tuple-element.126, f32[1024]{0:T(1024)S(1)} %fusion.23, ...), kind=kOutput, calls=%fused_computation.2.clone.1 | convolution fusion | flops 1621098496 | bytes 5780480 | tf_op jit(solution)/shard_map/while/body/eval_jaxpr/dot_general | solution.py:15
  119.5 8.4 %fusion.10 = f32[2048,128]{1,0:T(8,128)S(1)} fusion(bf16[2048,4096]{1,0:T(8,128)(2,1)} %param.10, bf16[4096,128]{1,0:T(8,128)(2,1)} %all-gather.2.cloned.1.call-done), kind=kOutput, calls=%fused_computation.28 | convolution fusion | flops 2147483648 | bytes 18874368 | tf_op jit(solution)/shard_map/dot_general | solution.py:46
  127.9 41.5 %all-reduce.10 = bf16[2048,128]{1,0:T(8,128)(2,1)S(1)} all-reduce(f32[2048,128]{1,0:T(8,128)S(1)} %fusion.10), channel_id=1, replica_groups=mesh['rows'=4,'cent'=8] {'rows'}, use_global_device_ids=true, to_apply=%region_8.9 | all-reduce | flops 262144 | bytes 1572864 | tf_op jit(solution)/shard_map/psum | solution.py:51
  169.5 8.2 %fusion.4 = f32[4,1024,128]{2,1,0:T(8,128)S(1)} fusion(bf16[4,1024,2048]{2,1,0:T(8,128)(2,1)} %get-tuple-element.58, bf16[2048,128]{1,0:T(8,128)(2,1)S(1)} %all-reduce.10), kind=kOutput, calls=%fused_computation.12 | convolution fusion | flops 2147483648 | bytes 19398656 | tf_op jit(solution)/shard_map/kbc,cd->kbd/dot_general | solution.py:28
  177.6 56.6 %all-reduce.11 = bf16[4096,128]{1,0:T(8,128)(2,1)S(1)} all-reduce(f32[4096,128]{1,0:T(8,128)S(1)} %bitcast.34), channel_id=1, replica_groups=mesh['rows'=4,'cent'=8] {'cent'}, use_global_device_ids=true, to_apply=%region_9.10 | all-reduce | flops 524288 | bytes 3145728 | tf_op jit(solution)/shard_map/psum | solution.py:54
  234.2 9.2 %convolution_bitcast_fusion.1 = f32[2048,128]{1,0:T(8,128)} fusion(bf16[4,1024,2048]{2,1,0:T(8,128)(2,1)} %get-tuple-element.58, bf16[4,1024,128]{2,1,0:T(8,128)(2,1)S(1)} %bitcast.35), kind=kOutput, calls=%fused_computation.9 | convolution fusion | flops 2147483648 | bytes 18874368 | tf_op jit(solution)/shard_map/kbc,kbd->cd/dot_general | solution.py:33
  243.5 50.6 %all-reduce.9.cloned.1.call-done = f32[2048,128]{1,0:T(8,128)} async-done(((f32[2048,128]{1,0:T(8,128)}), f32[2048,128]{1,0:T(8,128)}) %all-reduce.9.cloned.1.call-update) | async-done | bytes 1048592 | tf_op jit(solution)/shard_map/psum | solution.py:57
  294.0 9.8 %convolution_bitcast_fusion = f32[4096,128]{0,1:T(8,128)} fusion(bf16[2048,4096]{1,0:T(8,128)(2,1)} %param.10, f32[2048,128]{1,0:T(8,128)} %all-reduce.9.cloned.1.call-done), kind=kOutput, calls=%fused_computation.8 | convolution fusion | flops 2148007936 | bytes 19922944 | tf_op jit(solution)/shard_map/dot_general | solution.py:61
  304.8 39.4 %reduce-scatter.2.cloned.1.call-done = f32[512,128]{0,1:T(8,128)} async-done(((f32[4096,128]{0,1:T(8,128)}), f32[512,128]{0,1:T(8,128)}) %reduce-scatter.2.cloned.1.call-update) | async-done | bytes 262160 | tf_op jit(solution)/shard_map/reduce_scatter | solution.py:60
  344.2 1.6 multiply_reduce_fusion.2
  346.0 12.4 %all-reduce.1 = (f32[]{:T(128)}, f32[]{:T(128)}) all-reduce(f32[]{:T(128)} %multiply_reduce_fusion.3, f32[]{:T(128)} %multiply_reduce_fusion.2), channel_id=1, replica_groups=mesh['rows'=4,'cent'=8] {'rows'}, use_global_device_ids=true, to_apply=%region_1.2 | all-reduce | flops 2 | bytes 16 | tf_op jit(solution)/shard_map/psum | solution.py:70
  358.4 12.4 %all-reduce = (f32[]{:T(128)}, f32[]{:T(128)}) all-reduce(f32[]{:T(128)} %get-tuple-element.74, f32[]{:T(128)} %get-tuple-element.75), channel_id=1, replica_groups=mesh['rows'=4,'cent'=8] {'cent'}, use_global_device_ids=true, to_apply=%region_2.3 | all-reduce | flops 2 | bytes 16 | tf_op jit(solution)/shard_map/psum | solution.py:69
  372.1 1.6 multiply_reduce_fusion.1
  373.8 37.0 %psum.71 = f32[]{:T(128)} all-reduce(f32[]{:T(128)} %get-tuple-element.76), channel_id=1, replica_groups=mesh['rows'=4,'cent'=8] {'rows','cent'}, use_global_device_ids=true, to_apply=%region_16.17 | all-reduce | flops 1 | bytes 8 | tf_op jit(solution)/shard_map/psum | solution.py:75
  (30 shorter events, 6.1 us)
Async XLA Ops:
  8.0 64.9 %all-reduce.7.cloned.1.call-start = ((), (), s32[]{:S(2)}) async-start(), calls=%async_computation.1 | async-start | bytes 2097152 | tf_op jit(solution)/shard_map/psum | solution.py:43
  18.1 101.4 %all-gather.2.cloned.1.call-start = ((), (), s32[]{:S(2)}) async-start(), calls=%async_computation.2 | async-start | bytes 1179648 | tf_op jit(solution)/shard_map/all_gather | solution.py:48
  19.8 274.2 %all-reduce.9.cloned.1.call-start = ((), (), s32[]{:S(2)}) async-start(), calls=%async_computation.3 | async-start | bytes 2097152 | tf_op jit(solution)/shard_map/psum | solution.py:57
  243.4 60.5 %copy-start = (f32[512,128]{1,0:T(8,128)S(1)}, f32[512,128]{1,0:T(8,128)}, u32[]{:S(2)}) copy-start(f32[512,128]{1,0:T(8,128)} %param.13) | copy-start | bytes 786436
  243.4 60.7 %copy-start.1 = (f32[512,128]{1,0:T(8,128)S(1)}, f32[512,128]{1,0:T(8,128)}, u32[]{:S(2)}) copy-start(f32[512,128]{1,0:T(8,128)} %param.12) | copy-start | bytes 786436
  243.4 102.5 %copy-start.2 = (f32[512,128]{1,0:T(8,128)S(1)}, f32[512,128]{1,0:T(8,128)}, u32[]{:S(2)}) copy-start(f32[512,128]{1,0:T(8,128)} %param.11) | copy-start | bytes 786436
  243.4 100.8 %reduce-scatter.2.cloned.1.call-start = ((), (), s32[]{:S(2)}) async-start(), calls=%async_computation.4 | async-start | bytes 2359296 | tf_op jit(solution)/shard_map/reduce_scatter | solution.py:60
Sparse Core Ops, SparseCore 0:
  18.2 54.6 all-reduce.6
  243.5 50.4 all-reduce.8
Sparse Core Ops, SparseCore 1:
  21.1 25.9 all-gather.1
  304.0 40.2 reduce-scatter.1
